TPU v7x, 32 devices: a whole 2x2x4 slice. The times are simulated.
32 devices in a mesh: ccd: 4 (over z), tile: 8 (over y, x, core).
Axes of the slice: x: 2, y: 2, z: 4, core: 2. Of those that a mesh axis runs over, the one named last changes fastest.
Arguments:
- frames: bfloat16 [256, 512, 128], P(None, ('ccd', 'tile')), may hold values from -24 to 24
- source_mask: int32 [256, 512, 128], P(None, ('ccd', 'tile')), may hold values 0 or 1
- good_pixels: int32 [512, 128], P(('ccd', 'tile')), may hold values 0 or 1
Outputs:
- factor: float32 [256, 256], replicated
- basis: bfloat16 [256, 512, 128], P(None, ('ccd', 'tile'))
All inputs are finite; a program needn't handle non-finite values. No bound on the sum of `source_mask` or of `good_pixels` on one device may be relied on, other than what follows from the above.
Results may differ from a plain program's by a relative error of at most 0.00065.
Values may be sent and summed in bfloat16 or wider, within the bound.
A program may use at most 64 MiB of HBM per device.

v0:
```python
import jax
import jax.numpy as jnp
from jax import lax
from jax.sharding import PartitionSpec as P

REACH = 16


def padded_2(array, sides, width):
    for axis, dim in sides:
        peers, length = (lax.axis_size(axis), array.shape[dim])
        up = [(i, (i + 1) % peers) for i in range(peers - 1)]
        down = [(j, i) for i, j in up]
        last = lax.slice_in_dim(array, length - width, length, axis=dim)
        first = lax.slice_in_dim(array, 0, width, axis=dim)
        before = lax.ppermute(last, axis, up)
        after = lax.ppermute(first, axis, down)
        array = jnp.concatenate([before, array, after], axis=dim)
    return array


def tap_weight(distance):
    offsets = jnp.arange(-REACH, REACH + 1).astype(jnp.float32)
    norm_sum = jnp.sqrt(jnp.sum(jnp.exp(-2.0 * jnp.abs(offsets) / 6.0)))
    inside = jnp.abs(distance) <= REACH
    return jnp.where(inside, jnp.exp(-jnp.abs(distance).astype(jnp.float32) / 6.0) / norm_sum, 0.0)


def row_matrix(tile_rows):
    out_rows = jnp.arange(tile_rows).reshape(tile_rows, 1)
    in_rows = jnp.arange(tile_rows + 2 * REACH).reshape(1, tile_rows + 2 * REACH)
    return tap_weight(in_rows - out_rows - REACH)


def column_matrix(tile_cols):
    in_cols = jnp.arange(tile_cols).reshape(tile_cols, 1)
    out_cols = jnp.arange(tile_cols).reshape(1, tile_cols)
    return tap_weight(in_cols - out_cols)


def along_rows(padded, weights):
    return jnp.einsum(
        "ip,epw->eiw",
        weights,
        padded,
        precision=lax.Precision.HIGHEST,
        preferred_element_type=jnp.float32,
    )


def along_columns(block, weights):
    return jnp.einsum(
        "eiv,vw->eiw",
        block,
        weights,
        precision=lax.Precision.HIGHEST,
        preferred_element_type=jnp.float32,
    )


def local_gram(flat):
    return jnp.einsum(
        "ep,fp->ef", flat, flat, precision=lax.Precision.HIGHEST, preferred_element_type=jnp.float32
    )


def global_factor(flat, pixel_total):
    partial_value = local_gram(flat)
    gram = lax.psum(partial_value, ("ccd", "tile")) / pixel_total
    return jnp.linalg.cholesky(gram).T


def solve_upper(factor, flat):
    return lax.linalg.triangular_solve(factor.T, flat, left_side=True, lower=True)


def per_device(frames, source_mask, good_pixels):
    exposures, tile_rows, tile_cols = frames.shape
    masked = frames * source_mask.astype(jnp.bfloat16) * good_pixels.astype(jnp.bfloat16)[None]
    rows_weights = row_matrix(tile_rows)
    cols_weights = column_matrix(tile_cols)
    padded = padded_2(masked, ((("ccd", "tile"), 1),), REACH)
    smoothed = along_columns(along_rows(padded.astype(jnp.float32), rows_weights), cols_weights)
    flat = smoothed.reshape(exposures, tile_rows * tile_cols)
    pixel_total = float(tile_rows * tile_cols * lax.axis_size("ccd") * lax.axis_size("tile"))
    factor = global_factor(flat, pixel_total)
    solved = solve_upper(factor, flat)
    basis = solved.astype(jnp.bfloat16).reshape(exposures, tile_rows, tile_cols)
    return (factor, basis)


def solution(mesh):
    in_specs = (
        P(None, ("ccd", "tile"), None),
        P(None, ("ccd", "tile"), None),
        P(("ccd", "tile"), None),
    )
    out_specs = (P(), P(None, ("ccd", "tile"), None))
    return jax.shard_map(
        per_device, mesh=mesh, in_specs=in_specs, out_specs=out_specs, check_vma=False
    )
```

profile of v0, /device:TPU:0, one launch (start us, length us, event | category | flops | bytes accessed | tf_op | source)
XLA Modules:
  0.0 251.2 jit_solution(9715754093910273296)
XLA Ops:
  7.2 0.0 all-reduce.3.cloned.1.call-start
  7.2 0.7 convert_element_type.20
  7.9 2.1 multiply_multiply_fusion
  10.0 2.5 collective-permute-start
  12.5 1.3 collective-permute-start.1
  13.8 0.6 exponential_reduce_fusion
  15.1 0.0 collective-permute-done
  15.1 3.9 %collective-permute-done.1 = bf16[256,16,128]{2,1,0:T(8,128)(2,1)S(1)} collective-permute-done((bf16[256,16,128]{2,1,0:T(8,128)(2,1)S(1)}, bf16[256,16,128]{2,1,0:T(8,128)(2,1)S(1)}, u32[]{:S(2)}, u32[]{:S(2)}) %collective-permute-start.1) | collective-permute-done | bytes 1048608 | tf_op jit(solution)/shard_map/ppermute | solution.py:17
  19.1 1.4 fusion
  20.5 2.6 %fusion.7 = f32[256,16,128]{0,2,1:T(8,128)S(1)} fusion(f32[256,128,16]{1,2,0:T(8,128)S(1)} %fusion, f32[]{:T(128)S(6)} %sqrt.4), kind=kOutput, calls=%fused_computation.10 | convolution fusion | flops 805437440 | bytes 4194308 | tf_op jit(solution)/shard_map/eiv,vw->eiw/dot_general | solution.py:52
  23.1 4.2 %convolution_bitcast_fusion = f32[256,256]{0,1:T(8,128)} fusion(f32[256,16,128]{0,2,1:T(8,128)S(1)} %fusion.7), kind=kOutput, calls=%fused_computation.14 | convolution fusion | flops 1610612736 | bytes 2359296 | tf_op jit(solution)/shard_map/ep,fp->ef/dot_general | solution.py:62
  27.2 0.0 all-reduce.3.cloned.1.call-update
  27.3 1.2 fusion.54
  28.5 1.6 copy.10
  30.1 144.5 %all-reduce.3.cloned.1.call-done = f32[256,256]{0,1:T(8,128)} async-done(((f32[256,256]{0,1:T(8,128)}), f32[256,256]{0,1:T(8,128)}) %all-reduce.3.cloned.1.call-update) | async-done | bytes 262160 | tf_op jit(solution)/shard_map/psum | solution.py:69
  174.6 1.0 broadcast_multiply_fusion
  175.5 0.1 copy.9
  175.7 1.0 fusion.10
  176.7 11.7 %cholesky.49 = f32[128,128]{1,0:T(8,128)S(1)} custom-call(f32[128,128]{1,0:T(8,128)S(1)} %cholesky.115), custom_call_target="Cholesky" | custom-call | tf_op jit(solution)/shard_map/jit(cholesky)/cholesky | solution.py:70
  188.4 9.9 %custom-call.14 = f32[1,128,128]{1,2,0:T(8,128)S(1)} custom-call(f32[1,128,128]{2,1,0:T(8,128)S(1)} %get-tuple-element.29), custom_call_target="InvertDiagBlocksLowerTriangular" | custom-call | tf_op jit(solution)/shard_map/jit(cholesky)/cholesky | solution.py:70
  198.4 0.2 constant_dynamic-update-slice_fusion.1
  198.6 0.3 convolution_subtract_fusion.1
  198.8 11.7 %cholesky.102 = f32[128,128]{1,0:T(8,128)S(1)} custom-call(f32[128,128]{1,0:T(8,128)S(1)} %convolution_subtract_fusion.1), custom_call_target="Cholesky" | custom-call | tf_op jit(solution)/shard_map/jit(cholesky)/cholesky | solution.py:70
  210.6 0.6 compare_reduce_fusion
  212.5 0.7 fusion.11
  213.3 0.1 triangular_solve.52
  213.4 4.1 %while.1 = (s32[]{:T(128)}, f32[256,256]{1,0:T(8,128)S(1)}, s32[2,2]{1,0:T(2,128)S(1)}, f32[2,128,128]{2,1,0:T(8,128)S(1)}, s32[]{:T(128)}) while((s32[]{:T(128)}, f32[256,256]{1,0:T(8,128)S(1)}, s32[2,2]{1,0:T(2,128)S(1)}, f32[2,128,128]{2,1,0:T(8,128)S(1)}, s32[]{:T(128)}) %tuple.30), condition=%wide.while_cond, body=%wide.while_body.sunk | while | flops 2 | bytes 131181 | solution.py:74
  213.4 0.6 fusion.63
  214.0 1.4 bitcast_dynamic-update-slice_fusion.2
  215.4 0.6 fusion.63
  216.0 1.4 bitcast_dynamic-update-slice_fusion.2
  217.5 19.9 %custom-call.15 = f32[2,128,128]{1,2,0:T(8,128)S(1)} custom-call(f32[2,128,128]{2,1,0:T(8,128)S(1)} %get-tuple-element.9), custom_call_target="InvertDiagBlocksLowerTriangular" | custom-call | tf_op jit(solution)/shard_map/triangular_solve | solution.py:74
  237.4 1.1 fusion.14
  238.4 0.9 copy_bitcast_fusion
  239.3 1.0 fusion.6
  240.4 0.0 copy-start
  240.4 0.3 copy.25
  240.7 1.1 convolution_convert_fusion
  241.8 0.0 copy-done
  241.8 0.0 copy-start.1
  241.8 0.1 pad_maximum_fusion
  241.9 1.6 copy.15
  243.6 0.0 copy-done.1
  243.6 0.8 copy.14
  (8 shorter events, 0.1 us)
Async XLA Ops:
  7.2 167.4 %all-reduce.3.cloned.1.call-start = ((), (), s32[]{:S(2)}) async-start(), calls=%async_computation | async-start | bytes 524288 | tf_op jit(solution)/shard_map/psum | solution.py:69
  10.0 5.1 %collective-permute-start = (bf16[256,16,128]{2,1,0:T(8,128)(2,1)S(1)}, bf16[256,16,128]{2,1,0:T(8,128)(2,1)S(1)}, u32[]{:S(2)}, u32[]{:S(2)}) collective-permute-start(bf16[256,16,128]{2,1,0:T(8,128)(2,1)S(1)} %multiply_multiply_fusion), channel_id=1, source_target_pairs={{0,1},{1,2},{2,3},{3,4},{4,5},{5,6},{6,7},{7,8},{8,9},{9,10},{10,1... | collective-permute-start | bytes 3145736 | tf_op jit(solution)/shard_map/ppermute | solution.py:16
  12.5 6.6 %collective-permute-start.1 = (bf16[256,16,128]{2,1,0:T(8,128)(2,1)S(1)}, bf16[256,16,128]{2,1,0:T(8,128)(2,1)S(1)}, u32[]{:S(2)}, u32[]{:S(2)}) collective-permute-start(bf16[256,16,128]{2,1,0:T(8,128)(2,1)S(1)} %multiply_multiply_fusion), channel_id=1, source_target_pairs={{1,0},{2,1},{3,2},{4,3},{5,4},{6,5},{7,6},{8,7},{9,8},{10,9},{11,1... | collective-permute-start | bytes 3145736 | tf_op jit(solution)/shard_map/ppermute | solution.py:17
  240.4 1.4 copy-start
  241.8 1.8 copy-start.1
Sparse Core Ops, SparseCore 0:
  27.4 147.1 all-reduce.2
where the time goes:
time: 252 us; the launch traced here: 251 us
  waiting for transfers between devices  148 us (59%)
  other arithmetic  61 us (24%)
  between operations  16.2 us (6%)
  matrix products  11.8 us (5%)
  local copies, waits for them, and re-layouts  9.88 us (4%)
  starting transfers between devices  3.79 us (2%)
    psum x1, waiting for transfers between devices, global_factor(): gram = lax.psum(partial_value, ('ccd', 'tile')) / pixel_total  145 us
    another operation x6, other arithmetic, global_factor(): return jnp.linalg.cholesky(gram).T  34 us
    another operation x5, other arithmetic, solve_upper(): lax.linalg.triangular_solve(factor.T, flat, left_side=True, lower=True)  21.6 us
  transfers between devices with their start and end apart: 3, of which 2 were waited for; matrix products, arithmetic and copies ran while one was open for 1% of the time, Pallas kernels for 0%

commit v1 on v0

--- a/solution.py
+++ b/solution.py
@@ -1,9 +1,16 @@
+import functools
+
 import jax
 import jax.numpy as jnp
 from jax import lax
+from jax.experimental import pallas as pl
+from jax.experimental.pallas import tpu as pltpu
 from jax.sharding import PartitionSpec as P
 
 REACH = 16
+MESH = pl.DeviceIdType.MESH
+HIGH = lax.Precision.HIGHEST
+LANES = 128
 
 
 def padded_2(array, sides, width):
@@ -40,38 +47,164 @@
 
 def along_rows(padded, weights):
     return jnp.einsum(
-        "ip,epw->eiw",
-        weights,
-        padded,
-        precision=lax.Precision.HIGHEST,
-        preferred_element_type=jnp.float32,
+        "ip,epw->eiw", weights, padded, precision=HIGH, preferred_element_type=jnp.float32
     )
 
 
 def along_columns(block, weights):
     return jnp.einsum(
-        "eiv,vw->eiw",
-        block,
-        weights,
-        precision=lax.Precision.HIGHEST,
-        preferred_element_type=jnp.float32,
+        "eiv,vw->eiw", block, weights, precision=HIGH, preferred_element_type=jnp.float32
     )
 
 
 def local_gram(flat):
-    return jnp.einsum(
-        "ep,fp->ef", flat, flat, precision=lax.Precision.HIGHEST, preferred_element_type=jnp.float32
-    )
-
-
-def global_factor(flat, pixel_total):
-    partial_value = local_gram(flat)
-    gram = lax.psum(partial_value, ("ccd", "tile")) / pixel_total
-    return jnp.linalg.cholesky(gram).T
-
-
-def solve_upper(factor, flat):
-    return lax.linalg.triangular_solve(factor.T, flat, left_side=True, lower=True)
+    return jnp.einsum("ep,fp->ef", flat, flat, precision=HIGH, preferred_element_type=jnp.float32)
+
+
+def sum_kernel(ccds, tiles, p_ref, o_ref, near, far, whole, s1, r1, s2, r2, s3, r3):
+    c, t = lax.axis_index("ccd"), lax.axis_index("tile")
+    barrier = pltpu.get_barrier_semaphore()
+    for d in range(1, tiles):
+        pl.semaphore_signal(barrier, inc=1, device_id=(c, lax.rem(t + d, tiles)), device_id_type=MESH)
+    for d in range(1, ccds):
+        pl.semaphore_signal(barrier, inc=1, device_id=(lax.rem(c + d, ccds), t), device_id_type=MESH)
+    pl.semaphore_wait(barrier, tiles + ccds - 2)
+    first = []
+    for d in range(1, tiles):
+        peer = lax.rem(t + d, tiles)
+        copy = pltpu.make_async_remote_copy(
+            src_ref=p_ref.at[peer], dst_ref=near.at[d - 1], send_sem=s1.at[d - 1], recv_sem=r1.at[d - 1],
+            device_id=(c, peer), device_id_type=MESH)
+        copy.start()
+        first.append(copy)
+    total = p_ref[t]
+    for d in range(1, tiles):
+        first[d - 1].wait_recv()
+        total = total + near[d - 1]
+    far[c] = total
+    second = []
+    for d in range(1, ccds):
+        copy = pltpu.make_async_remote_copy(
+            src_ref=far.at[c], dst_ref=far.at[c], send_sem=s2.at[d - 1], recv_sem=r2.at[d - 1],
+            device_id=(lax.rem(c + d, ccds), t), device_id_type=MESH)
+        copy.start()
+        second.append(copy)
+    for copy in second:
+        copy.wait_recv()
+    total = far[0]
+    for i in range(1, ccds):
+        total = total + far[i]
+    whole[t] = total
+    third = []
+    for d in range(1, tiles):
+        copy = pltpu.make_async_remote_copy(
+            src_ref=whole.at[t], dst_ref=whole.at[t], send_sem=s3.at[d - 1], recv_sem=r3.at[d - 1],
+            device_id=(c, lax.rem(t + d, tiles)), device_id_type=MESH)
+        copy.start()
+        third.append(copy)
+    for copy in third:
+        copy.wait_recv()
+    o_ref[...] = whole[...]
+    for copy in first + second + third:
+        copy.wait_send()
+
+
+def total_over_devices(parts):
+    ccds, tiles = lax.axis_size("ccd"), lax.axis_size("tile")
+    rows = parts.shape[1]
+    dma = pltpu.SemaphoreType.DMA
+    return pl.pallas_call(
+        functools.partial(sum_kernel, ccds, tiles),
+        out_shape=jax.ShapeDtypeStruct(parts.shape, jnp.float32),
+        in_specs=[pl.BlockSpec(memory_space=pltpu.VMEM)],
+        out_specs=pl.BlockSpec(memory_space=pltpu.VMEM),
+        scratch_shapes=[
+            pltpu.VMEM((tiles - 1, rows, LANES), jnp.float32),
+            pltpu.VMEM((ccds, rows, LANES), jnp.float32),
+            pltpu.VMEM((tiles, rows, LANES), jnp.float32),
+            dma((tiles - 1,)), dma((tiles - 1,)),
+            dma((ccds - 1,)), dma((ccds - 1,)),
+            dma((tiles - 1,)), dma((tiles - 1,)),
+        ],
+        compiler_params=pltpu.CompilerParams(collective_id=0, has_side_effects=True),
+    )(parts)
+
+
+def matmul(a, b, contract=(1, 0)):
+    return lax.dot_general(
+        a, b, (((contract[0],), (contract[1],)), ((), ())), precision=HIGH, preferred_element_type=jnp.float32
+    )
+
+
+def factor_block(block, rows_ref):
+    groups = LANES // 8
+    live = [block[8 * g:8 * g + 8, :] for g in range(groups)]
+    lane = lax.broadcasted_iota(jnp.int32, (8, LANES), 1)
+    sub = lax.broadcasted_iota(jnp.int32, (8, LANES), 0)
+    for j in range(LANES):
+        g, s = divmod(j, 8)
+        row = jnp.broadcast_to(live[g][s:s + 1, :], (8, LANES))
+        pivot = jnp.broadcast_to(row[:, j:j + 1], (8, LANES))
+        at = lane == j
+        inv = 1.0 / pivot
+        scaled = jnp.where(at, inv, row * inv)
+        for i in range(g, groups):
+            if i == g and s == 7:
+                continue
+            mult = jnp.broadcast_to(live[i][:, j:j + 1], (8, LANES))
+            new = jnp.where(at, 0.0, live[i]) - mult * scaled
+            live[i] = jnp.where(sub > s, new, live[i]) if i == g else new
+        root = lax.rsqrt(pivot)
+        root = root * (1.5 - 0.5 * pivot * root * root)
+        rows_ref[j:j + 1, :] = (row * root)[:1, :]
+    done = rows_ref[...]
+    row_id = lax.broadcasted_iota(jnp.int32, (LANES, LANES), 0)
+    col_id = lax.broadcasted_iota(jnp.int32, (LANES, LANES), 1)
+    upper = jnp.where(col_id >= row_id, done, 0.0)
+    inverse = jnp.where(col_id < row_id, done, jnp.where(col_id == row_id, 1.0 / done, 0.0))
+    return upper, inverse
+
+
+def solve_kernel(g_ref, a_ref, f_ref, b_ref, rows_ref, x_ref, out32):
+    h = LANES
+    upper, inv1 = factor_block(g_ref[0], rows_ref)
+    f_ref[:h, :h] = upper
+    f_ref[h:, :h] = jnp.zeros((h, h), jnp.float32)
+    low = matmul(g_ref[1], inv1, (1, 1))
+    f_ref[:h, h:] = low.T
+    rest = g_ref[2] - matmul(low, low, (1, 1))
+    upper, inv2 = factor_block(rest, rows_ref)
+    f_ref[h:, h:] = upper
+    x_ref[:h, :h] = inv1
+    x_ref[:h, h:] = jnp.zeros((h, h), jnp.float32)
+    x_ref[h:, h:] = inv2
+    x_ref[h:, :h] = -matmul(inv2, matmul(low, inv1))
+    exposures, pixels = a_ref.shape
+    tile_rows = pixels // LANES
+    for k in range(tile_rows // 2):
+        part = matmul(x_ref[...], a_ref[:, 2 * k * LANES:2 * (k + 1) * LANES])
+        for i in range(2):
+            out32[pl.ds(2 * k + i, exposures, stride=tile_rows), :] = part[:, i * LANES:(i + 1) * LANES]
+    b_ref[...] = out32[...].astype(jnp.bfloat16)
+
+
+def solve(gram, flat):
+    exposures, pixels = flat.shape
+    vm = pl.BlockSpec(memory_space=pltpu.VMEM)
+    return pl.pallas_call(
+        solve_kernel,
+        out_shape=(
+            jax.ShapeDtypeStruct((exposures, exposures), jnp.float32),
+            jax.ShapeDtypeStruct((exposures * pixels // LANES, LANES), jnp.bfloat16),
+        ),
+        in_specs=[vm, vm],
+        out_specs=(vm, vm),
+        scratch_shapes=[
+            pltpu.VMEM((LANES, LANES), jnp.float32),
+            pltpu.VMEM((exposures, exposures), jnp.float32),
+            pltpu.VMEM((exposures * pixels // LANES, LANES), jnp.float32),
+        ],
+    )(gram, flat)
 
 
 def per_device(frames, source_mask, good_pixels):
@@ -82,11 +215,14 @@
     padded = padded_2(masked, ((("ccd", "tile"), 1),), REACH)
     smoothed = along_columns(along_rows(padded.astype(jnp.float32), rows_weights), cols_weights)
     flat = smoothed.reshape(exposures, tile_rows * tile_cols)
-    pixel_total = float(tile_rows * tile_cols * lax.axis_size("ccd") * lax.axis_size("tile"))
-    factor = global_factor(flat, pixel_total)
-    solved = solve_upper(factor, flat)
-    basis = solved.astype(jnp.bfloat16).reshape(exposures, tile_rows, tile_cols)
-    return (factor, basis)
+    tiles = lax.axis_size("tile")
+    pixel_total = float(tile_rows * tile_cols * lax.axis_size("ccd") * tiles)
+    part = local_gram(flat)
+    packed = jnp.stack([part[:LANES, :LANES], part[LANES:, :LANES], part[LANES:, LANES:]])
+    summed = total_over_devices(packed.reshape(tiles, 3 * LANES // tiles, LANES))
+    gram = summed.reshape(3, LANES, LANES) / pixel_total
+    factor, basis = solve(gram, flat)
+    return (factor, basis.reshape(exposures, tile_rows, tile_cols))
 
 
 def solution(mesh):

time: 252 us -> 103 us (0.41)
  waiting for transfers between devices: 148 us -> 0.89 us
  Pallas kernels: 0 us -> 80.9 us
  other arithmetic: 61 us -> 5.74 us
  between operations: 16.2 us -> 1.39 us
  local copies, waits for them, and re-layouts: 9.88 us -> 1.88 us
  matrix products: 11.8 us -> 7.47 us
    psum x1 -> x0, waiting for transfers between devices: 145 us -> none  [global_factor(): gram = lax.psum(partial_value, ('ccd', 'tile')) / pixel_total]
    pallas_call x0 -> x2, Pallas kernels: none -> 80.9 us  [the longest x1 40.6 us: total_over_devices(): pl.pallas_call(functools.partial(sum_kernel, ccds, tiles), out_shape=jax....]
    another operation x11 -> x1, other arithmetic: 55.7 us -> 0.69 us  [per_device(): jnp.stack([part[:LANES, :LANES], part[LANES:, :LANES], part[LANES:, LANES...]
    another operation x12 -> x1, local copies, waits for them, and re-layouts: 7.25 us -> 0.02 us  [per_device(): jnp.stack([part[:LANES, :LANES], part[LANES:, :LANES], part[LANES:, LANES...]
    ppermute x1, waiting for transfers between devices: 3.94 us -> 0.01 us  [padded_2(): after = lax.ppermute(first, axis, down)]
    another operation x5 -> x0, matrix products: 3.64 us -> none  [the longest x3 3.17 us: solve_upper(): lax.linalg.triangular_solve(factor.T, flat, left_side=True, lower=True)]
  transfers between devices with their start and end apart: 3 -> 2, of which waited for: 2 -> 1; matrix products, arithmetic and copies ran while one was open for 1% -> 1% of each run, Pallas kernels for 0% -> 0%
where the time goes in v1:
time: 103 us
  Pallas kernels  80.9 us (79%)
  matrix products  7.47 us (7%)
  other arithmetic  5.74 us (6%)
  starting transfers between devices  4.39 us (4%)
  local copies, waits for them, and re-layouts  1.88 us (2%)
  between operations  1.39 us (1%)
    pallas_call x1, Pallas kernels, total_over_devices(): pl.pallas_call(functools.partial(sum_kernel, ccds, tiles), out_shape=jax....  40.6 us
    pallas_call x1, Pallas kernels, solve(): pl.pallas_call(solve_kernel, out_shape=(jax.ShapeDtypeStruct((exposures,...  40.3 us
    dot_general x1, matrix products, local_gram(): jnp.einsum('ep,fp->ef', flat, flat, precision=HIGH, preferred_element_typ...  3.48 us
    ppermute x1, starting transfers between devices, padded_2(): before = lax.ppermute(last, axis, up)  3.1 us
    dot_general x1, matrix products, along_columns(): jnp.einsum('eiv,vw->eiw', block, weights, precision=HIGH, preferred_eleme...  2.58 us
    mul x1, other arithmetic, per_device(): frames * source_mask.astype(jnp.bfloat16)  2.1 us
  transfers between devices with their start and end apart: 2, of which 1 were waited for; matrix products, arithmetic and copies ran while one was open for 1% of the time, Pallas kernels for 0%

profile of v1, /device:TPU:0, one launch (start us, length us, event | category | flops | bytes accessed | tf_op | source)
XLA Modules:
  0.0 102.6 jit_solution(5991086245622198793)
XLA Ops:
  0.6 0.7 convert_element_type.18
  1.3 2.1 %multiply_multiply_fusion = bf16[256,16,128]{2,1,0:T(8,128)(2,1)S(1)} fusion(bf16[256,16,128]{2,1,0:T(8,128)(2,1)} %param.3, s32[256,16,128]{2,1,0:T(8,128)} %param.4, bf16[16,128]{1,0:T(8,128)(2,1)S(1)} %convert_element_type.18), kind=kLoop, calls=%fused_computation.10 | loop fusion | flops 1572864 | bytes 4198400 | tf_op jit(solution)/shard_map/mul | solution.py:212
  3.4 1.3 %collective-permute-start.1 = (bf16[256,16,128]{2,1,0:T(8,128)(2,1)S(1)}, bf16[256,16,128]{2,1,0:T(8,128)(2,1)S(1)}, u32[]{:S(2)}, u32[]{:S(2)}) collective-permute-start(bf16[256,16,128]{2,1,0:T(8,128)(2,1)S(1)} %multiply_multiply_fusion), channel_id=1, source_target_pairs={{1,0},{2,1},{3,2},{4,3},{5,4},{6,5},{7,6},{8,7},{9,8},{10,9},{11,1... | collective-permute-start | bytes 3145736 | tf_op jit(solution)/shard_map/ppermute | solution.py:24
  4.7 3.1 %collective-permute-start = (bf16[256,16,128]{2,1,0:T(8,128)(2,1)S(1)}, bf16[256,16,128]{2,1,0:T(8,128)(2,1)S(1)}, u32[]{:S(2)}, u32[]{:S(2)}) collective-permute-start(bf16[256,16,128]{2,1,0:T(8,128)(2,1)S(1)} %multiply_multiply_fusion), channel_id=1, source_target_pairs={{0,1},{1,2},{2,3},{3,4},{4,5},{5,6},{6,7},{7,8},{8,9},{9,10},{10,1... | collective-permute-start | bytes 3145736 | tf_op jit(solution)/shard_map/ppermute | solution.py:23
  7.8 0.6 exponential_reduce_fusion
  9.1 0.0 collective-permute-done.1
  9.2 0.9 collective-permute-done
  10.0 1.4 %fusion = f32[256,128,16]{1,2,0:T(8,128)S(1)} fusion(bf16[256,16,128]{2,1,0:T(8,128)(2,1)S(1)} %collective-permute-done.1, bf16[256,16,128]{2,1,0:T(8,128)(2,1)S(1)} %multiply_multiply_fusion, bf16[256,16,128]{2,1,0:T(8,128)(2,1)S(1)} %collective-permute-done, f32[]{:T(128)S(6)} %sqrt.4), kind=kOutput, calls=%fused_computation | convolution fusion | flops 311433984 | bytes 5242884 | tf_op jit(solution)/shard_map/ip,epw->eiw/dot_general | solution.py:49
  11.4 2.6 %fusion.6 = f32[256,16,128]{0,2,1:T(8,128)S(1)} fusion(f32[256,128,16]{1,2,0:T(8,128)S(1)} %fusion, f32[]{:T(128)S(6)} %sqrt.4), kind=kOutput, calls=%fused_computation.6 | convolution fusion | flops 805437440 | bytes 4194308 | tf_op jit(solution)/shard_map/eiv,vw->eiw/dot_general | solution.py:55
  14.0 3.5 %convolution_bitcast_fusion = f32[256,256]{1,0:T(8,128)S(1)} fusion(f32[256,16,128]{0,2,1:T(8,128)S(1)} %fusion.6), kind=kOutput, calls=%fused_computation.9 | convolution fusion | flops 1610612736 | bytes 2359296 | tf_op jit(solution)/shard_map/ep,fp->ef/dot_general | solution.py:61
  17.5 0.7 pad_maximum_fusion
  18.2 40.6 %shard_map.50 = f32[8,48,128]{2,1,0:T(8,128)} custom-call(f32[8,48,128]{2,1,0:T(8,128)} %bitcast.25), custom_call_target="tpu_custom_call" | custom-call | tf_op jit(solution)/shard_map/pallas_call | solution.py:116
  58.8 1.6 %broadcast_multiply_fusion = f32[8,48,128]{2,1,0:T(8,128)} fusion(f32[8,48,128]{2,1,0:T(8,128)} %shard_map.50), kind=kLoop, calls=%fused_computation.12 | loop fusion | flops 49152 | bytes 393216 | tf_op jit(solution)/shard_map/div | solution.py:223
  60.4 1.9 %copy.11.a_ref = f32[256,2048]{1,0:T(8,128)} copy(f32[256,2048]{0,1:T(8,128)S(1)} %bitcast.23) | data formatting | bytes 4194304 | tf_op jit(solution)/shard_map/reshape | solution.py:217
  62.3 40.3 %shard_map.51 = (f32[256,256]{1,0:T(8,128)}, bf16[4096,128]{1,0:T(8,128)(2,1)}) custom-call(f32[3,128,128]{2,1,0:T(8,128)} %bitcast.24, f32[256,2048]{1,0:T(8,128)} %copy.11.a_ref), custom_call_target="tpu_custom_call" | custom-call | tf_op jit(solution)/shard_map/pallas_call | solution.py:194
  (1 shorter events, 0.0 us)
Async XLA Ops:
  3.4 5.7 %collective-permute-start.1 = (bf16[256,16,128]{2,1,0:T(8,128)(2,1)S(1)}, bf16[256,16,128]{2,1,0:T(8,128)(2,1)S(1)}, u32[]{:S(2)}, u32[]{:S(2)}) collective-permute-start(bf16[256,16,128]{2,1,0:T(8,128)(2,1)S(1)} %multiply_multiply_fusion), channel_id=1, source_target_pairs={{1,0},{2,1},{3,2},{4,3},{5,4},{6,5},{7,6},{8,7},{9,8},{10,9},{11,1... | collective-permute-start | bytes 3145736 | tf_op jit(solution)/shard_map/ppermute | solution.py:24
  4.7 5.3 %collective-permute-start = (bf16[256,16,128]{2,1,0:T(8,128)(2,1)S(1)}, bf16[256,16,128]{2,1,0:T(8,128)(2,1)S(1)}, u32[]{:S(2)}, u32[]{:S(2)}) collective-permute-start(bf16[256,16,128]{2,1,0:T(8,128)(2,1)S(1)} %multiply_multiply_fusion), channel_id=1, source_target_pairs={{0,1},{1,2},{2,3},{3,4},{4,5},{5,6},{6,7},{7,8},{8,9},{9,10},{10,1... | collective-permute-start | bytes 3145736 | tf_op jit(solution)/shard_map/ppermute | solution.py:23

commit v2 on v1

v2 whole, which is shorter than its diff:
```python
import functools
import math

import jax
import jax.numpy as jnp
from jax import lax
from jax.experimental import pallas as pl
from jax.experimental.pallas import tpu as pltpu
from jax.sharding import PartitionSpec as P

REACH = 16
MESH = pl.DeviceIdType.MESH
HIGH = lax.Precision.HIGHEST
LANES = 128


def tap_weight(distance):
    offsets = jnp.arange(-REACH, REACH + 1).astype(jnp.float32)
    norm_sum = jnp.sqrt(jnp.sum(jnp.exp(-2.0 * jnp.abs(offsets) / 6.0)))
    inside = jnp.abs(distance) <= REACH
    return jnp.where(inside, jnp.exp(-jnp.abs(distance).astype(jnp.float32) / 6.0) / norm_sum, 0.0)


def column_matrix(tile_cols):
    in_cols = jnp.arange(tile_cols).reshape(tile_cols, 1)
    out_cols = jnp.arange(tile_cols).reshape(1, tile_cols)
    weights = tap_weight(in_cols - out_cols)
    offsets = jnp.arange(-REACH, REACH + 1).astype(jnp.float32)
    return weights / jnp.sqrt(jnp.sum(jnp.exp(-2.0 * jnp.abs(offsets) / 6.0)))


def sum_kernel(ccds, tiles, p_ref, o_ref, near, far, whole, s1, r1, s2, r2, s3, r3):
    c, t = lax.axis_index("ccd"), lax.axis_index("tile")
    barrier = pltpu.get_barrier_semaphore()
    for d in range(1, tiles):
        pl.semaphore_signal(barrier, inc=1, device_id=(c, lax.rem(t + d, tiles)), device_id_type=MESH)
    for d in range(1, ccds):
        pl.semaphore_signal(barrier, inc=1, device_id=(lax.rem(c + d, ccds), t), device_id_type=MESH)
    pl.semaphore_wait(barrier, tiles + ccds - 2)
    first = []
    for d in range(1, tiles):
        peer = lax.rem(t + d, tiles)
        copy = pltpu.make_async_remote_copy(
            src_ref=p_ref.at[peer], dst_ref=near.at[d - 1], send_sem=s1.at[d - 1], recv_sem=r1.at[d - 1],
            device_id=(c, peer), device_id_type=MESH)
        copy.start()
        first.append(copy)
    total = p_ref[t]
    for d in range(1, tiles):
        first[d - 1].wait_recv()
        total = total + near[d - 1]
    far[c] = total
    second = []
    for d in range(1, ccds):
        copy = pltpu.make_async_remote_copy(
            src_ref=far.at[c], dst_ref=far.at[c], send_sem=s2.at[d - 1], recv_sem=r2.at[d - 1],
            device_id=(lax.rem(c + d, ccds), t), device_id_type=MESH)
        copy.start()
        second.append(copy)
    for copy in second:
        copy.wait_recv()
    total = far[0]
    for i in range(1, ccds):
        total = total + far[i]
    whole[t] = total
    third = []
    for d in range(1, tiles):
        copy = pltpu.make_async_remote_copy(
            src_ref=whole.at[t], dst_ref=whole.at[t], send_sem=s3.at[d - 1], recv_sem=r3.at[d - 1],
            device_id=(c, lax.rem(t + d, tiles)), device_id_type=MESH)
        copy.start()
        third.append(copy)
    for copy in third:
        copy.wait_recv()
    o_ref[...] = whole[...]
    for copy in first + second + third:
        copy.wait_send()


def total_over_devices(parts):
    ccds, tiles = lax.axis_size("ccd"), lax.axis_size("tile")
    rows = parts.shape[1]
    dma = pltpu.SemaphoreType.DMA
    return pl.pallas_call(
        functools.partial(sum_kernel, ccds, tiles),
        out_shape=jax.ShapeDtypeStruct(parts.shape, jnp.float32),
        in_specs=[pl.BlockSpec(memory_space=pltpu.VMEM)],
        out_specs=pl.BlockSpec(memory_space=pltpu.VMEM),
        scratch_shapes=[
            pltpu.VMEM((tiles - 1, rows, LANES), jnp.float32),
            pltpu.VMEM((ccds, rows, LANES), jnp.float32),
            pltpu.VMEM((tiles, rows, LANES), jnp.float32),
            dma((tiles - 1,)), dma((tiles - 1,)),
            dma((ccds - 1,)), dma((ccds - 1,)),
            dma((tiles - 1,)), dma((tiles - 1,)),
        ],
        compiler_params=pltpu.CompilerParams(collective_id=0, has_side_effects=True),
    )(parts)


def matmul(a, b, contract=(1, 0)):
    return lax.dot_general(
        a, b, (((contract[0],), (contract[1],)), ((), ())), precision=HIGH, preferred_element_type=jnp.float32
    )


def factor_block(block, rows_ref):
    groups = LANES // 8
    full = (8, LANES)
    live = [block[8 * g:8 * g + 8, :] for g in range(groups)]
    lane = lax.broadcasted_iota(jnp.int32, full, 1)
    for g in range(groups):
        base = 8 * g
        inside = jnp.logical_and(lane >= base, lane < base + 8)
        cols = [jnp.broadcast_to(live[g][:, base + k:base + k + 1], full) for k in range(8)]
        small = {(j, k): jnp.broadcast_to(cols[k][j:j + 1, :], full) for j in range(8) for k in range(j, 8)}
        rows = []
        for k in range(8):
            row = jnp.broadcast_to(live[g][k:k + 1, :], full)
            rows.append(jnp.where(inside, jnp.where(lane == base + k, 1.0, 0.0), row))
        inv, lower = [], {}
        for j in range(8):
            inv.append(1.0 / small[j, j])
            for k in range(j + 1, 8):
                for m in range(k, 8):
                    small[k, m] = small[k, m] - (small[j, k] * small[j, m]) * inv[j]
            for k in range(j + 1, 8):
                lower[k, j] = small[j, k] * inv[j]
                rows[k] = rows[k] - lower[k, j] * rows[j]
        for j in range(8):
            pivot = small[j, j]
            root = lax.rsqrt(pivot)
            root = root * (1.5 - 0.5 * pivot * root * root)
            out = rows[j]
            for m in range(j, 8):
                out = jnp.where(lane == base + m, small[j, m], out)
            rows_ref[base + j:base + j + 1, :] = (out * root)[:1, :]
        if g == groups - 1:
            break
        back = [rows[k] * inv[k] for k in range(8)]
        for k in range(7, -1, -1):
            for m in range(k):
                back[m] = back[m] - lower[k, m] * back[k]
        for i in range(g + 1, groups):
            total = None
            for k in range(8):
                term = jnp.broadcast_to(live[i][:, base + k:base + k + 1], full) * back[k]
                total = term if total is None else total + term
            live[i] = jnp.where(inside, 0.0, live[i]) - total
    done = rows_ref[...]
    row_id = lax.broadcasted_iota(jnp.int32, (LANES, LANES), 0)
    col_id = lax.broadcasted_iota(jnp.int32, (LANES, LANES), 1)
    upper = jnp.where(col_id >= row_id, done, 0.0)
    inverse = jnp.where(col_id < row_id, done, jnp.where(col_id == row_id, 1.0 / done, 0.0))
    return upper, inverse


def split(value):
    high = value.astype(jnp.bfloat16)
    return high, (value - high.astype(jnp.float32)).astype(jnp.bfloat16)


def product(a, b, contract):
    return lax.dot_general(
        a, b, (((contract[0],), (contract[1],)), ((), ())), preferred_element_type=jnp.float32
    )


def smooth_rows(read, rows):
    decay = math.exp(-1.0 / 6.0)
    tail = math.exp(-(REACH + 1) / 6.0)
    ahead = read(0)
    for p in range(1, REACH + 1):
        ahead = ahead * decay + read(p)
    out = [ahead]
    for i in range(1, rows):
        ahead = ahead * decay + (read(REACH + i) - tail * read(i - 1))
        out.append(ahead)
    last = REACH + rows - 1
    back = read(last + REACH) * decay
    for k in range(REACH - 1, 0, -1):
        back = (back + read(last + k)) * decay
    out[rows - 1] = out[rows - 1] + back
    for i in range(rows - 2, -1, -1):
        p = REACH + i
        back = (back + read(p + 1)) * decay - tail * read(p + REACH + 1)
        out[i] = out[i] + back
    return out


def smooth_kernel(tile_rows, before_ref, own_ref, after_ref, w_ref, hi_ref, lo_ref, g_ref, pad, done):
    pad[0] = before_ref[...].astype(jnp.float32)
    pad[1] = own_ref[...].astype(jnp.float32)
    pad[2] = after_ref[...].astype(jnp.float32)
    exposures = hi_ref.shape[0]
    step = 32

    @pl.loop(0, exposures // step)
    def _(c):
        def read(p):
            return pad[p // tile_rows, pl.ds(c * (step * tile_rows) + p % tile_rows, step, stride=tile_rows), :]

        here = pl.multiple_of(c * step, step)
        for r, value in enumerate(smooth_rows(read, tile_rows)):
            done[r, pl.ds(here, step), :] = value

    for r in range(tile_rows):
        hi, lo = split(matmul(done[r], w_ref[...]))
        hi_ref[:, r * LANES:(r + 1) * LANES] = hi
        lo_ref[:, r * LANES:(r + 1) * LANES] = lo
    h = LANES
    cross = product(hi_ref[...], lo_ref[...], (1, 1))
    gram = product(hi_ref[...], hi_ref[...], (1, 1)) + product(lo_ref[...], lo_ref[...], (1, 1))
    gram = gram + (cross + cross.T)
    g_ref[0] = gram[:h, :h]
    g_ref[1] = gram[h:, :h]
    g_ref[2] = gram[h:, h:]


def smooth(before, own, after, weights, tile_rows):
    exposures = own.shape[0] // tile_rows
    pixels = tile_rows * LANES
    vm = pl.BlockSpec(memory_space=pltpu.VMEM)
    return pl.pallas_call(
        functools.partial(smooth_kernel, tile_rows),
        out_shape=(
            jax.ShapeDtypeStruct((exposures, pixels), jnp.bfloat16),
            jax.ShapeDtypeStruct((exposures, pixels), jnp.bfloat16),
            jax.ShapeDtypeStruct((3, LANES, LANES), jnp.float32),
        ),
        in_specs=[vm] * 4,
        out_specs=(vm,) * 3,
        scratch_shapes=[
            pltpu.VMEM((3,) + own.shape, jnp.float32),
            pltpu.VMEM((tile_rows, exposures, LANES), jnp.float32),
        ],
    )(before, own, after, weights)


def solve_kernel(pixel_total, g_ref, hi_ref, lo_ref, f_ref, b_ref, rows_ref, xh_ref, xl_ref, out32):
    h = LANES
    scale = 1.0 / pixel_total
    upper, inv1 = factor_block(g_ref[0] * scale, rows_ref)
    f_ref[:h, :h] = upper
    f_ref[h:, :h] = jnp.zeros((h, h), jnp.float32)
    low = matmul(g_ref[1] * scale, inv1, (1, 1))
    f_ref[:h, h:] = low.T
    rest = g_ref[2] * scale - matmul(low, low, (1, 1))
    upper, inv2 = factor_block(rest, rows_ref)
    f_ref[h:, h:] = upper
    xh_ref[:h, :h], xl_ref[:h, :h] = split(inv1)
    xh_ref[:h, h:] = jnp.zeros((h, h), jnp.bfloat16)
    xl_ref[:h, h:] = jnp.zeros((h, h), jnp.bfloat16)
    xh_ref[h:, h:], xl_ref[h:, h:] = split(inv2)
    xh_ref[h:, :h], xl_ref[h:, :h] = split(-matmul(inv2, matmul(low, inv1)))
    exposures, pixels = hi_ref.shape
    tile_rows = pixels // LANES
    for k in range(tile_rows // 2):
        at = slice(2 * k * LANES, 2 * (k + 1) * LANES)
        hi, lo = hi_ref[:, at], lo_ref[:, at]
        part = product(xh_ref[...], hi, (1, 0)) + (
            product(xh_ref[...], lo, (1, 0)) + product(xl_ref[...], hi, (1, 0)) + product(xl_ref[...], lo, (1, 0)))
        for i in range(2):
            out32[pl.ds(2 * k + i, exposures, stride=tile_rows), :] = part[:, i * LANES:(i + 1) * LANES]
    b_ref[...] = out32[...].astype(jnp.bfloat16)


def solve(gram, hi, lo, pixel_total):
    exposures, pixels = hi.shape
    vm = pl.BlockSpec(memory_space=pltpu.VMEM)
    return pl.pallas_call(
        functools.partial(solve_kernel, pixel_total),
        out_shape=(
            jax.ShapeDtypeStruct((exposures, exposures), jnp.float32),
            jax.ShapeDtypeStruct((exposures * pixels // LANES, LANES), jnp.bfloat16),
        ),
        in_specs=[vm, vm, vm],
        out_specs=(vm, vm),
        scratch_shapes=[
            pltpu.VMEM((LANES, LANES), jnp.float32),
            pltpu.VMEM((exposures, exposures), jnp.bfloat16),
            pltpu.VMEM((exposures, exposures), jnp.bfloat16),
            pltpu.VMEM((exposures * pixels // LANES, LANES), jnp.float32),
        ],
    )(gram, hi, lo)


def shift_rows(masked, axes):
    peers = lax.axis_size(axes)
    up = [(i, (i + 1) % peers) for i in range(peers - 1)]
    down = [(j, i) for i, j in up]
    return lax.ppermute(masked, axes, up), lax.ppermute(masked, axes, down)


def per_device(frames, source_mask, good_pixels):
    exposures, tile_rows, tile_cols = frames.shape
    masked = frames * source_mask.astype(jnp.bfloat16) * good_pixels.astype(jnp.bfloat16)[None]
    masked = masked.reshape(exposures * tile_rows, tile_cols)
    before, after = shift_rows(masked, ("ccd", "tile"))
    tiles = lax.axis_size("tile")
    pixel_total = float(tile_rows * tile_cols * lax.axis_size("ccd") * tiles)
    hi, lo, packed = smooth(before, masked, after, column_matrix(tile_cols), tile_rows)
    summed = total_over_devices(packed.reshape(tiles, 3 * LANES // tiles, LANES))
    factor, basis = solve(summed.reshape(3, LANES, LANES), hi, lo, pixel_total)
    return (factor, basis.reshape(exposures, tile_rows, tile_cols))


def solution(mesh):
    in_specs = (
        P(None, ("ccd", "tile"), None),
        P(None, ("ccd", "tile"), None),
        P(("ccd", "tile"), None),
    )
    out_specs = (P(), P(None, ("ccd", "tile"), None))
    return jax.shard_map(
        per_device, mesh=mesh, in_specs=in_specs, out_specs=out_specs, check_vma=False
    )
```

time: 103 us -> 75.3 us (0.73)
  Pallas kernels: 80.9 us -> 63.3 us
  matrix products: 7.47 us -> 0 us
  other arithmetic: 5.74 us -> 4.07 us
    pallas_call x1 -> x2, Pallas kernels: 40.3 us -> 23.5 us  [the longest x1 15.1 us: solve(): pl.pallas_call(functools.partial(solve_kernel, pixel_total), out_shape=(j...]
    dot_general x3 -> x0, matrix products: 7.47 us -> none  [the longest x1 3.48 us: local_gram(): jnp.einsum('ep,fp->ef', flat, flat, precision=HIGH, preferred_element_typ...]
    reshape x1 -> x0, local copies, waits for them, and re-layouts: 1.86 us -> none  [per_device(): flat = smoothed.reshape(exposures, tile_rows * tile_cols)]
    unnamed x0 -> x6, local copies, waits for them, and re-layouts: none -> 1.72 us
  transfers between devices with their start and end apart: 2 -> 2, of which waited for: 1 -> 1; matrix products, arithmetic and copies ran while one was open for 1% -> 2% of each run, Pallas kernels for 0% -> 0%
where the time goes in v2:
time: 75.3 us; the launch traced here: 75.1 us
  Pallas kernels  63.3 us (84%)
  starting transfers between devices  4.39 us (6%)
  other arithmetic  4.07 us (5%)
  local copies, waits for them, and re-layouts  1.72 us (2%)
  between operations  1.36 us (2%)
    pallas_call x1, Pallas kernels, total_over_devices(): pl.pallas_call(functools.partial(sum_kernel, ccds, tiles), out_shape=jax....  39.8 us
    pallas_call x1, Pallas kernels, solve(): pl.pallas_call(functools.partial(solve_kernel, pixel_total), out_shape=(j...  15.1 us
    pallas_call x1, Pallas kernels, smooth(): pl.pallas_call(functools.partial(smooth_kernel, tile_rows), out_shape=(ja...  8.35 us
    ppermute x2, starting transfers between devices, shift_rows(): return (lax.ppermute(masked, axes, up), lax.ppermute(masked, axes, down))  4.39 us
    mul x1, other arithmetic, per_device(): frames * source_mask.astype(jnp.bfloat16)  2.1 us
    unnamed x6, local copies, waits for them, and re-layouts  1.72 us
  transfers between devices with their start and end apart: 2, of which 1 were waited for; matrix products, arithmetic and copies ran while one was open for 2% of the time, Pallas kernels for 0%

profile of v2, /device:TPU:0, one launch (start us, length us, event | category | flops | bytes accessed | tf_op | source)
XLA Modules:
  0.0 75.1 jit_solution(859224431776303126)
XLA Ops:
  0.6 0.7 convert_element_type.14
  1.3 2.1 %multiply_multiply_fusion = bf16[256,16,128]{2,1,0:T(8,128)(2,1)S(1)} fusion(bf16[256,16,128]{2,1,0:T(8,128)(2,1)} %param.3, s32[256,16,128]{2,1,0:T(8,128)} %param.4, bf16[16,128]{1,0:T(8,128)(2,1)S(1)} %convert_element_type.14), kind=kLoop, calls=%fused_computation | loop fusion | flops 1572864 | bytes 4198400 | tf_op jit(solution)/shard_map/mul | solution.py:297
  3.4 0.0 copy-start
  3.4 1.3 %collective-permute-start.1 = (bf16[4096,128]{1,0:T(8,128)(2,1)S(1)}, bf16[4096,128]{1,0:T(8,128)(2,1)S(1)}, u32[]{:S(2)}, u32[]{:S(2)}) collective-permute-start(bf16[4096,128]{1,0:T(8,128)(2,1)S(1)} %bitcast.4), channel_id=1, source_target_pairs={{1,0},{2,1},{3,2},{4,3},{5,4},{6,5},{7,6},{8,7},{9,8},{10,9},{11,1... | collective-permute-start | bytes 3145736 | tf_op jit(solution)/shard_map/ppermute | solution.py:292
  4.7 3.1 %collective-permute-start = (bf16[4096,128]{1,0:T(8,128)(2,1)S(1)}, bf16[4096,128]{1,0:T(8,128)(2,1)S(1)}, u32[]{:S(2)}, u32[]{:S(2)}) collective-permute-start(bf16[4096,128]{1,0:T(8,128)(2,1)S(1)} %bitcast.5), channel_id=1, source_target_pairs={{0,1},{1,2},{2,3},{3,4},{4,5},{5,6},{6,7},{7,8},{8,9},{9,10},{10,1... | collective-permute-start | bytes 3145736 | tf_op jit(solution)/shard_map/ppermute | solution.py:292
  7.8 0.6 exponential_reduce_fusion
  9.2 0.7 select_divide_fusion.w_ref
  9.8 0.0 collective-permute-done.1.after_ref
  9.8 0.0 copy-start.1
  9.8 0.2 collective-permute-done.before_ref
  10.0 0.0 copy-done
  10.0 0.8 copy-done.1
  10.8 0.0 copy-start.2
  10.8 1.0 %copy-done.2 = bf16[4096,128]{1,0:T(8,128)(2,1)} copy-done((bf16[4096,128]{1,0:T(8,128)(2,1)}, bf16[4096,128]{1,0:T(8,128)(2,1)S(1)}, u32[]{:S(2)}) %copy-start.2) | copy-done | bytes 1048600
  11.8 8.3 %shard_map.50 = (bf16[256,2048]{1,0:T(8,128)(2,1)}, bf16[256,2048]{1,0:T(8,128)(2,1)}, f32[3,128,128]{2,1,0:T(8,128)}) custom-call(bf16[4096,128]{1,0:T(8,128)(2,1)} %copy-done.2, bf16[4096,128]{1,0:T(8,128)(2,1)} %bitcast.6, bf16[4096,128]{1,0:T(8,128)(2,1)} %copy-done.1, f32[128,128]{1,0:T(8,128)} %select_divide_fusion.w_ref), custom_call_target="tpu_custom_call" | custom-call | tf_op jit(solution)/shard_map/pallas_call | solution.py:224
  20.1 39.8 %shard_map.51 = f32[8,48,128]{2,1,0:T(8,128)} custom-call(f32[8,48,128]{2,1,0:T(8,128)} %bitcast.8), custom_call_target="tpu_custom_call" | custom-call | tf_op jit(solution)/shard_map/pallas_call | solution.py:84
  59.9 15.1 %shard_map.52 = (f32[256,256]{1,0:T(8,128)}, bf16[4096,128]{1,0:T(8,128)(2,1)}) custom-call(f32[3,128,128]{2,1,0:T(8,128)} %bitcast.7, bf16[256,2048]{1,0:T(8,128)(2,1)} %get-tuple-element.8.hi_ref, bf16[256,2048]{1,0:T(8,128)(2,1)} %get-tuple-element.9.lo_ref), custom_call_target="tpu_custom_call" | custom-call | tf_op jit(solution)/shard_map/pallas_call | solution.py:271
Async XLA Ops:
  3.4 6.6 %copy-start = (bf16[256,16,128]{2,1,0:T(8,128)(2,1)}, bf16[256,16,128]{2,1,0:T(8,128)(2,1)S(1)}, u32[]{:S(2)}) copy-start(bf16[256,16,128]{2,1,0:T(8,128)(2,1)S(1)} %multiply_multiply_fusion) | copy-start | bytes 3145732
  3.4 6.4 %collective-permute-start.1 = (bf16[4096,128]{1,0:T(8,128)(2,1)S(1)}, bf16[4096,128]{1,0:T(8,128)(2,1)S(1)}, u32[]{:S(2)}, u32[]{:S(2)}) collective-permute-start(bf16[4096,128]{1,0:T(8,128)(2,1)S(1)} %bitcast.4), channel_id=1, source_target_pairs={{1,0},{2,1},{3,2},{4,3},{5,4},{6,5},{7,6},{8,7},{9,8},{10,9},{11,1... | collective-permute-start | bytes 3145736 | tf_op jit(solution)/shard_map/ppermute | solution.py:292
  4.7 5.3 %collective-permute-start = (bf16[4096,128]{1,0:T(8,128)(2,1)S(1)}, bf16[4096,128]{1,0:T(8,128)(2,1)S(1)}, u32[]{:S(2)}, u32[]{:S(2)}) collective-permute-start(bf16[4096,128]{1,0:T(8,128)(2,1)S(1)} %bitcast.5), channel_id=1, source_target_pairs={{0,1},{1,2},{2,3},{3,4},{4,5},{5,6},{6,7},{7,8},{8,9},{9,10},{10,1... | collective-permute-start | bytes 3145736 | tf_op jit(solution)/shard_map/ppermute | solution.py:292
  9.8 1.0 %copy-start.1 = (bf16[4096,128]{1,0:T(8,128)(2,1)}, bf16[4096,128]{1,0:T(8,128)(2,1)S(1)}, u32[]{:S(2)}) copy-start(bf16[4096,128]{1,0:T(8,128)(2,1)S(1)} %collective-permute-done.1.after_ref) | copy-start | bytes 3145732
  10.8 1.0 %copy-start.2 = (bf16[4096,128]{1,0:T(8,128)(2,1)}, bf16[4096,128]{1,0:T(8,128)(2,1)S(1)}, u32[]{:S(2)}) copy-start(bf16[4096,128]{1,0:T(8,128)(2,1)S(1)} %collective-permute-done.before_ref) | copy-start | bytes 3145732

commit v3 on v2

--- a/solution.py
+++ b/solution.py
@@ -27,75 +27,6 @@
     weights = tap_weight(in_cols - out_cols)
     offsets = jnp.arange(-REACH, REACH + 1).astype(jnp.float32)
     return weights / jnp.sqrt(jnp.sum(jnp.exp(-2.0 * jnp.abs(offsets) / 6.0)))
-
-
-def sum_kernel(ccds, tiles, p_ref, o_ref, near, far, whole, s1, r1, s2, r2, s3, r3):
-    c, t = lax.axis_index("ccd"), lax.axis_index("tile")
-    barrier = pltpu.get_barrier_semaphore()
-    for d in range(1, tiles):
-        pl.semaphore_signal(barrier, inc=1, device_id=(c, lax.rem(t + d, tiles)), device_id_type=MESH)
-    for d in range(1, ccds):
-        pl.semaphore_signal(barrier, inc=1, device_id=(lax.rem(c + d, ccds), t), device_id_type=MESH)
-    pl.semaphore_wait(barrier, tiles + ccds - 2)
-    first = []
-    for d in range(1, tiles):
-        peer = lax.rem(t + d, tiles)
-        copy = pltpu.make_async_remote_copy(
-            src_ref=p_ref.at[peer], dst_ref=near.at[d - 1], send_sem=s1.at[d - 1], recv_sem=r1.at[d - 1],
-            device_id=(c, peer), device_id_type=MESH)
-        copy.start()
-        first.append(copy)
-    total = p_ref[t]
-    for d in range(1, tiles):
-        first[d - 1].wait_recv()
-        total = total + near[d - 1]
-    far[c] = total
-    second = []
-    for d in range(1, ccds):
-        copy = pltpu.make_async_remote_copy(
-            src_ref=far.at[c], dst_ref=far.at[c], send_sem=s2.at[d - 1], recv_sem=r2.at[d - 1],
-            device_id=(lax.rem(c + d, ccds), t), device_id_type=MESH)
-        copy.start()
-        second.append(copy)
-    for copy in second:
-        copy.wait_recv()
-    total = far[0]
-    for i in range(1, ccds):
-        total = total + far[i]
-    whole[t] = total
-    third = []
-    for d in range(1, tiles):
-        copy = pltpu.make_async_remote_copy(
-            src_ref=whole.at[t], dst_ref=whole.at[t], send_sem=s3.at[d - 1], recv_sem=r3.at[d - 1],
-            device_id=(c, lax.rem(t + d, tiles)), device_id_type=MESH)
-        copy.start()
-        third.append(copy)
-    for copy in third:
-        copy.wait_recv()
-    o_ref[...] = whole[...]
-    for copy in first + second + third:
-        copy.wait_send()
-
-
-def total_over_devices(parts):
-    ccds, tiles = lax.axis_size("ccd"), lax.axis_size("tile")
-    rows = parts.shape[1]
-    dma = pltpu.SemaphoreType.DMA
-    return pl.pallas_call(
-        functools.partial(sum_kernel, ccds, tiles),
-        out_shape=jax.ShapeDtypeStruct(parts.shape, jnp.float32),
-        in_specs=[pl.BlockSpec(memory_space=pltpu.VMEM)],
-        out_specs=pl.BlockSpec(memory_space=pltpu.VMEM),
-        scratch_shapes=[
-            pltpu.VMEM((tiles - 1, rows, LANES), jnp.float32),
-            pltpu.VMEM((ccds, rows, LANES), jnp.float32),
-            pltpu.VMEM((tiles, rows, LANES), jnp.float32),
-            dma((tiles - 1,)), dma((tiles - 1,)),
-            dma((ccds - 1,)), dma((ccds - 1,)),
-            dma((tiles - 1,)), dma((tiles - 1,)),
-        ],
-        compiler_params=pltpu.CompilerParams(collective_id=0, has_side_effects=True),
-    )(parts)
 
 
 def matmul(a, b, contract=(1, 0)):
@@ -188,53 +119,144 @@
     return out
 
 
-def smooth_kernel(tile_rows, before_ref, own_ref, after_ref, w_ref, hi_ref, lo_ref, g_ref, pad, done):
-    pad[0] = before_ref[...].astype(jnp.float32)
-    pad[1] = own_ref[...].astype(jnp.float32)
-    pad[2] = after_ref[...].astype(jnp.float32)
+CHUNKS = 4
+
+
+def exchange_kernel(ccds, tiles, tile_rows, own_ref, w_ref, hi_ref, lo_ref, o_ref, halo, pad, done, mine,
+                    near, far, whole, hs, hr, s1, r1, s2, r2, s3, r3):
+    c, t = lax.axis_index("ccd"), lax.axis_index("tile")
+    me, total = c * tiles + t, ccds * tiles
+    after, before = lax.rem(me + 1, total), lax.rem(me + total - 1, total)
+    after_id = (lax.div(after, tiles), lax.rem(after, tiles))
+    before_id = (lax.div(before, tiles), lax.rem(before, tiles))
+    barrier = pltpu.get_barrier_semaphore()
+    for peer in (before_id, after_id):
+        pl.semaphore_signal(barrier, inc=1, device_id=peer, device_id_type=MESH)
+    for d in range(1, tiles):
+        pl.semaphore_signal(barrier, inc=1, device_id=(c, lax.rem(t + d, tiles)), device_id_type=MESH)
+    for d in range(1, ccds):
+        pl.semaphore_signal(barrier, inc=1, device_id=(lax.rem(c + d, ccds), t), device_id_type=MESH)
+    pl.semaphore_wait(barrier, tiles + ccds)
     exposures = hi_ref.shape[0]
-    step = 32
-
-    @pl.loop(0, exposures // step)
-    def _(c):
-        def read(p):
-            return pad[p // tile_rows, pl.ds(c * (step * tile_rows) + p % tile_rows, step, stride=tile_rows), :]
-
-        here = pl.multiple_of(c * step, step)
-        for r, value in enumerate(smooth_rows(read, tile_rows)):
-            done[r, pl.ds(here, step), :] = value
-
-    for r in range(tile_rows):
-        hi, lo = split(matmul(done[r], w_ref[...]))
-        hi_ref[:, r * LANES:(r + 1) * LANES] = hi
-        lo_ref[:, r * LANES:(r + 1) * LANES] = lo
+    part = exposures // CHUNKS
+    span = part * tile_rows
+    moves = []
+    for k in range(CHUNKS):
+        rows = pl.ds(k * span, span)
+        pair = []
+        for side, peer in enumerate((after_id, before_id)):
+            copy = pltpu.make_async_remote_copy(
+                src_ref=own_ref.at[rows], dst_ref=halo.at[side, rows], send_sem=hs.at[side, k],
+                recv_sem=hr.at[side, k], device_id=peer, device_id_type=MESH)
+            copy.start()
+            pair.append(copy)
+        moves.append(pair)
+    has_before = jnp.where(me > 0, 1.0, 0.0)
+    has_after = jnp.where(me < total - 1, 1.0, 0.0)
+    weights = w_ref[...]
     h = LANES
-    cross = product(hi_ref[...], lo_ref[...], (1, 1))
-    gram = product(hi_ref[...], hi_ref[...], (1, 1)) + product(lo_ref[...], lo_ref[...], (1, 1))
-    gram = gram + (cross + cross.T)
-    g_ref[0] = gram[:h, :h]
-    g_ref[1] = gram[h:, :h]
-    g_ref[2] = gram[h:, h:]
-
-
-def smooth(before, own, after, weights, tile_rows):
-    exposures = own.shape[0] // tile_rows
+    for k in range(CHUNKS):
+        rows = pl.ds(k * span, span)
+        pad[1] = own_ref[rows, :].astype(jnp.float32)
+        for copy in moves[k]:
+            copy.wait_recv()
+        pad[0] = halo[0, rows, :].astype(jnp.float32) * has_before
+        pad[2] = halo[1, rows, :].astype(jnp.float32) * has_after
+        step = 32
+
+        @pl.loop(0, part // step)
+        def _(n):
+            def read(p):
+                first = n * (step * tile_rows) + p % tile_rows
+                return pad[p // tile_rows, pl.ds(first, step, stride=tile_rows), :]
+
+            for r, value in enumerate(smooth_rows(read, tile_rows)):
+                done[pl.ds(pl.multiple_of(r * part + n * step, step), step), :] = value
+
+        hi, lo = split(matmul(done[...], weights))
+        for r in range(tile_rows):
+            hi_ref[k * part:(k + 1) * part, r * h:(r + 1) * h] = hi[r * part:(r + 1) * part]
+            lo_ref[k * part:(k + 1) * part, r * h:(r + 1) * h] = lo[r * part:(r + 1) * part]
+        if (k + 1) * part == h:
+            hi, lo = hi_ref[:h, :], lo_ref[:h, :]
+            cross = product(hi, lo, (1, 1))
+            first = product(hi, hi, (1, 1)) + product(lo, lo, (1, 1)) + (cross + cross.T)
+    hi, lo = hi_ref[h:, :], lo_ref[h:, :]
+    rest = product(hi, hi_ref[...], (1, 1)) + product(lo, lo_ref[...], (1, 1)) + (
+        product(hi, lo_ref[...], (1, 1)) + product(lo, hi_ref[...], (1, 1)))
+    packed = jnp.concatenate([first, rest[:, :h], rest[:, h:]], axis=0)
+    share = mine.shape[1]
+    for i in range(tiles):
+        mine[i] = packed[i * share:(i + 1) * share]
+    sent = []
+    for d in range(1, tiles):
+        peer = lax.rem(t + d, tiles)
+        copy = pltpu.make_async_remote_copy(
+            src_ref=mine.at[peer], dst_ref=near.at[d - 1], send_sem=s1.at[d - 1], recv_sem=r1.at[d - 1],
+            device_id=(c, peer), device_id_type=MESH)
+        copy.start()
+        sent.append(copy)
+    value = mine[t]
+    for d in range(1, tiles):
+        sent[d - 1].wait_recv()
+        value = value + near[d - 1]
+    far[c] = value
+    second = []
+    for d in range(1, ccds):
+        copy = pltpu.make_async_remote_copy(
+            src_ref=far.at[c], dst_ref=far.at[c], send_sem=s2.at[d - 1], recv_sem=r2.at[d - 1],
+            device_id=(lax.rem(c + d, ccds), t), device_id_type=MESH)
+        copy.start()
+        second.append(copy)
+    for copy in second:
+        copy.wait_recv()
+    value = far[0]
+    for i in range(1, ccds):
+        value = value + far[i]
+    whole[t] = value
+    third = []
+    for d in range(1, tiles):
+        copy = pltpu.make_async_remote_copy(
+            src_ref=whole.at[t], dst_ref=whole.at[t], send_sem=s3.at[d - 1], recv_sem=r3.at[d - 1],
+            device_id=(c, lax.rem(t + d, tiles)), device_id_type=MESH)
+        copy.start()
+        third.append(copy)
+    for copy in third:
+        copy.wait_recv()
+    o_ref[...] = whole[...]
+    for copy in sum(moves, []) + sent + second + third:
+        copy.wait_send()
+
+
+def exchange(masked, weights, tile_rows):
+    ccds, tiles = lax.axis_size("ccd"), lax.axis_size("tile")
+    exposures = masked.shape[0] // tile_rows
     pixels = tile_rows * LANES
+    share = 3 * LANES // tiles
+    dma = pltpu.SemaphoreType.DMA
     vm = pl.BlockSpec(memory_space=pltpu.VMEM)
+    split_shape = jax.ShapeDtypeStruct((exposures, pixels), jnp.bfloat16)
+    span = masked.shape[0] // CHUNKS
     return pl.pallas_call(
-        functools.partial(smooth_kernel, tile_rows),
-        out_shape=(
-            jax.ShapeDtypeStruct((exposures, pixels), jnp.bfloat16),
-            jax.ShapeDtypeStruct((exposures, pixels), jnp.bfloat16),
-            jax.ShapeDtypeStruct((3, LANES, LANES), jnp.float32),
-        ),
-        in_specs=[vm] * 4,
+        functools.partial(exchange_kernel, ccds, tiles, tile_rows),
+        out_shape=(split_shape, split_shape, jax.ShapeDtypeStruct((tiles, share, LANES), jnp.float32)),
+        in_specs=[vm, vm],
         out_specs=(vm,) * 3,
         scratch_shapes=[
-            pltpu.VMEM((3,) + own.shape, jnp.float32),
-            pltpu.VMEM((tile_rows, exposures, LANES), jnp.float32),
+            pltpu.VMEM((2,) + masked.shape, jnp.bfloat16),
+            pltpu.VMEM((3, span, LANES), jnp.float32),
+            pltpu.VMEM((span, LANES), jnp.float32),
+            pltpu.VMEM((tiles, share, LANES), jnp.float32),
+            pltpu.VMEM((tiles - 1, share, LANES), jnp.float32),
+            pltpu.VMEM((ccds, share, LANES), jnp.float32),
+            pltpu.VMEM((tiles, share, LANES), jnp.float32),
+            dma((2, CHUNKS)), dma((2, CHUNKS)),
+            dma((tiles - 1,)), dma((tiles - 1,)),
+            dma((ccds - 1,)), dma((ccds - 1,)),
+            dma((tiles - 1,)), dma((tiles - 1,)),
         ],
-    )(before, own, after, weights)
+        compiler_params=pltpu.CompilerParams(collective_id=0, has_side_effects=True),
+    )(masked, weights)
 
 
 def solve_kernel(pixel_total, g_ref, hi_ref, lo_ref, f_ref, b_ref, rows_ref, xh_ref, xl_ref, out32):
@@ -285,22 +307,13 @@
     )(gram, hi, lo)
 
 
-def shift_rows(masked, axes):
-    peers = lax.axis_size(axes)
-    up = [(i, (i + 1) % peers) for i in range(peers - 1)]
-    down = [(j, i) for i, j in up]
-    return lax.ppermute(masked, axes, up), lax.ppermute(masked, axes, down)
-
-
 def per_device(frames, source_mask, good_pixels):
     exposures, tile_rows, tile_cols = frames.shape
     masked = frames * source_mask.astype(jnp.bfloat16) * good_pixels.astype(jnp.bfloat16)[None]
     masked = masked.reshape(exposures * tile_rows, tile_cols)
-    before, after = shift_rows(masked, ("ccd", "tile"))
     tiles = lax.axis_size("tile")
     pixel_total = float(tile_rows * tile_cols * lax.axis_size("ccd") * tiles)
-    hi, lo, packed = smooth(before, masked, after, column_matrix(tile_cols), tile_rows)
-    summed = total_over_devices(packed.reshape(tiles, 3 * LANES // tiles, LANES))
+    hi, lo, summed = exchange(masked, column_matrix(tile_cols), tile_rows)
     factor, basis = solve(summed.reshape(3, LANES, LANES), hi, lo, pixel_total)
     return (factor, basis.reshape(exposures, tile_rows, tile_cols))
 

time: 75.3 us -> 70.6 us (0.938)
  starting transfers between devices: 4.39 us -> 0 us
  local copies, waits for them, and re-layouts: 1.72 us -> 0 us
  other arithmetic: 4.07 us -> 5.05 us
    ppermute x2 -> x0, starting transfers between devices: 4.39 us -> none  [shift_rows(): return (lax.ppermute(masked, axes, up), lax.ppermute(masked, axes, down))]
    unnamed x6 -> x0, local copies, waits for them, and re-layouts: 1.72 us -> none
    mul x1, other arithmetic: 2.1 us -> 3.06 us  [per_device(): frames * source_mask.astype(jnp.bfloat16)]
    pallas_call x2 -> x1, Pallas kernels: 48.1 us -> 48.9 us  [exchange(): pl.pallas_call(functools.partial(exchange_kernel, ccds, tiles, tile_rows)...]
  transfers between devices with their start and end apart: 2 -> 0, of which waited for: 1 -> 0; matrix products, arithmetic and copies ran while one was open for 2% -> 0% of each run, Pallas kernels for 0% -> 0%
where the time goes in v3:
time: 70.6 us; the launch traced here: 70.4 us
  Pallas kernels  64 us (91%)
  other arithmetic  5.05 us (7%)
  between operations  1.33 us (2%)
    pallas_call x1, Pallas kernels, exchange(): pl.pallas_call(functools.partial(exchange_kernel, ccds, tiles, tile_rows)...  48.9 us
    pallas_call x1, Pallas kernels, solve(): pl.pallas_call(functools.partial(solve_kernel, pixel_total), out_shape=(j...  15.1 us
    mul x1, other arithmetic, per_device(): frames * source_mask.astype(jnp.bfloat16)  3.06 us

profile of v3, /device:TPU:0, one launch (start us, length us, event | category | flops | bytes accessed | tf_op | source)
XLA Modules:
  0.0 70.4 jit_solution(7779583096117509450)
XLA Ops:
  0.6 0.6 exponential_reduce_fusion
  1.9 0.7 convert_element_type.14
  2.6 0.7 select_divide_fusion.w_ref
  3.3 3.1 %multiply_multiply_fusion = bf16[256,16,128]{2,1,0:T(8,128)(2,1)} fusion(bf16[256,16,128]{2,1,0:T(8,128)(2,1)} %param.3, s32[256,16,128]{2,1,0:T(8,128)} %param.4, bf16[16,128]{1,0:T(8,128)(2,1)S(1)} %convert_element_type.14), kind=kLoop, calls=%fused_computation | loop fusion | flops 1572864 | bytes 4198400 | tf_op jit(solution)/shard_map/mul | solution.py:312
  6.4 48.9 %shard_map.50 = (bf16[256,2048]{1,0:T(8,128)(2,1)}, bf16[256,2048]{1,0:T(8,128)(2,1)}, f32[8,48,128]{2,1,0:T(8,128)}) custom-call(bf16[4096,128]{1,0:T(8,128)(2,1)} %bitcast.3, f32[128,128]{1,0:T(8,128)} %select_divide_fusion.w_ref), custom_call_target="tpu_custom_call" | custom-call | tf_op jit(solution)/shard_map/pallas_call | solution.py:240
  55.3 15.1 %shard_map.51 = (f32[256,256]{1,0:T(8,128)}, bf16[4096,128]{1,0:T(8,128)(2,1)}) custom-call(f32[3,128,128]{2,1,0:T(8,128)} %bitcast.4, bf16[256,2048]{1,0:T(8,128)(2,1)} %get-tuple-element.8.hi_ref, bf16[256,2048]{1,0:T(8,128)(2,1)} %get-tuple-element.9.lo_ref), custom_call_target="tpu_custom_call" | custom-call | tf_op jit(solution)/shard_map/pallas_call | solution.py:293

commit v4 on v3

--- a/solution.py
+++ b/solution.py
@@ -3,6 +3,7 @@
 
 import jax
 import jax.numpy as jnp
+import numpy as np
 from jax import lax
 from jax.experimental import pallas as pl
 from jax.experimental.pallas import tpu as pltpu
@@ -14,19 +15,10 @@
 LANES = 128
 
 
-def tap_weight(distance):
-    offsets = jnp.arange(-REACH, REACH + 1).astype(jnp.float32)
-    norm_sum = jnp.sqrt(jnp.sum(jnp.exp(-2.0 * jnp.abs(offsets) / 6.0)))
-    inside = jnp.abs(distance) <= REACH
-    return jnp.where(inside, jnp.exp(-jnp.abs(distance).astype(jnp.float32) / 6.0) / norm_sum, 0.0)
-
-
 def column_matrix(tile_cols):
-    in_cols = jnp.arange(tile_cols).reshape(tile_cols, 1)
-    out_cols = jnp.arange(tile_cols).reshape(1, tile_cols)
-    weights = tap_weight(in_cols - out_cols)
-    offsets = jnp.arange(-REACH, REACH + 1).astype(jnp.float32)
-    return weights / jnp.sqrt(jnp.sum(jnp.exp(-2.0 * jnp.abs(offsets) / 6.0)))
+    distance = np.abs(np.arange(tile_cols)[:, None] - np.arange(tile_cols)[None, :])
+    norm = np.sum(np.exp(-2.0 * np.abs(np.arange(-REACH, REACH + 1)) / 6.0))
+    return np.where(distance <= REACH, np.exp(-distance / 6.0) / norm, 0.0).astype(np.float32)
 
 
 def matmul(a, b, contract=(1, 0)):
@@ -122,7 +114,7 @@
 CHUNKS = 4
 
 
-def exchange_kernel(ccds, tiles, tile_rows, own_ref, w_ref, hi_ref, lo_ref, o_ref, halo, pad, done, mine,
+def exchange_kernel(ccds, tiles, tile_rows, frame_ref, mask_ref, good_ref, w_ref, hi_ref, lo_ref, o_ref, own_ref, halo, pad, done, mine,
                     near, far, whole, hs, hr, s1, r1, s2, r2, s3, r3):
     c, t = lax.axis_index("ccd"), lax.axis_index("tile")
     me, total = c * tiles + t, ccds * tiles
@@ -130,19 +122,24 @@
     after_id = (lax.div(after, tiles), lax.rem(after, tiles))
     before_id = (lax.div(before, tiles), lax.rem(before, tiles))
     barrier = pltpu.get_barrier_semaphore()
+    good = good_ref[...].astype(jnp.float32)[None]
     for peer in (before_id, after_id):
         pl.semaphore_signal(barrier, inc=1, device_id=peer, device_id_type=MESH)
     for d in range(1, tiles):
         pl.semaphore_signal(barrier, inc=1, device_id=(c, lax.rem(t + d, tiles)), device_id_type=MESH)
     for d in range(1, ccds):
         pl.semaphore_signal(barrier, inc=1, device_id=(lax.rem(c + d, ccds), t), device_id_type=MESH)
-    pl.semaphore_wait(barrier, tiles + ccds)
     exposures = hi_ref.shape[0]
     part = exposures // CHUNKS
     span = part * tile_rows
     moves = []
     for k in range(CHUNKS):
         rows = pl.ds(k * span, span)
+        block = pl.ds(k * part, part)
+        value = frame_ref[block].astype(jnp.float32) * (mask_ref[block].astype(jnp.float32) * good)
+        own_ref[rows, :] = value.astype(jnp.bfloat16).reshape(span, LANES)
+        if k == 0:
+            pl.semaphore_wait(barrier, tiles + ccds)
         pair = []
         for side, peer in enumerate((after_id, before_id)):
             copy = pltpu.make_async_remote_copy(
@@ -228,22 +225,23 @@
         copy.wait_send()
 
 
-def exchange(masked, weights, tile_rows):
+def exchange(frames, source_mask, good_pixels, weights):
     ccds, tiles = lax.axis_size("ccd"), lax.axis_size("tile")
-    exposures = masked.shape[0] // tile_rows
+    exposures, tile_rows, _ = frames.shape
     pixels = tile_rows * LANES
     share = 3 * LANES // tiles
     dma = pltpu.SemaphoreType.DMA
     vm = pl.BlockSpec(memory_space=pltpu.VMEM)
     split_shape = jax.ShapeDtypeStruct((exposures, pixels), jnp.bfloat16)
-    span = masked.shape[0] // CHUNKS
+    span = exposures * tile_rows // CHUNKS
     return pl.pallas_call(
         functools.partial(exchange_kernel, ccds, tiles, tile_rows),
         out_shape=(split_shape, split_shape, jax.ShapeDtypeStruct((tiles, share, LANES), jnp.float32)),
-        in_specs=[vm, vm],
+        in_specs=[vm] * 4,
         out_specs=(vm,) * 3,
         scratch_shapes=[
-            pltpu.VMEM((2,) + masked.shape, jnp.bfloat16),
+            pltpu.VMEM((exposures * tile_rows, LANES), jnp.bfloat16),
+            pltpu.VMEM((2, exposures * tile_rows, LANES), jnp.bfloat16),
             pltpu.VMEM((3, span, LANES), jnp.float32),
             pltpu.VMEM((span, LANES), jnp.float32),
             pltpu.VMEM((tiles, share, LANES), jnp.float32),
@@ -256,7 +254,7 @@
             dma((tiles - 1,)), dma((tiles - 1,)),
         ],
         compiler_params=pltpu.CompilerParams(collective_id=0, has_side_effects=True),
-    )(masked, weights)
+    )(frames, source_mask, good_pixels, weights)
 
 
 def solve_kernel(pixel_total, g_ref, hi_ref, lo_ref, f_ref, b_ref, rows_ref, xh_ref, xl_ref, out32):
@@ -309,11 +307,9 @@
 
 def per_device(frames, source_mask, good_pixels):
     exposures, tile_rows, tile_cols = frames.shape
-    masked = frames * source_mask.astype(jnp.bfloat16) * good_pixels.astype(jnp.bfloat16)[None]
-    masked = masked.reshape(exposures * tile_rows, tile_cols)
     tiles = lax.axis_size("tile")
     pixel_total = float(tile_rows * tile_cols * lax.axis_size("ccd") * tiles)
-    hi, lo, summed = exchange(masked, column_matrix(tile_cols), tile_rows)
+    hi, lo, summed = exchange(frames, source_mask, good_pixels, column_matrix(tile_cols))
     factor, basis = solve(summed.reshape(3, LANES, LANES), hi, lo, pixel_total)
     return (factor, basis.reshape(exposures, tile_rows, tile_cols))
 

time: 70.6 us -> 65.4 us (0.926)
  other arithmetic: 5.05 us -> 0 us
    mul x1 -> x0, other arithmetic: 3.06 us -> none  [per_device(): frames * source_mask.astype(jnp.bfloat16)]
where the time goes in v4:
time: 65.4 us; the launch traced here: 65.3 us
  Pallas kernels  64.6 us (99%)
    pallas_call x1, Pallas kernels, exchange(): pl.pallas_call(functools.partial(exchange_kernel, ccds, tiles, tile_rows)...  49.5 us
    pallas_call x1, Pallas kernels, solve(): pl.pallas_call(functools.partial(solve_kernel, pixel_total), out_shape=(j...  15.1 us

profile of v4, /device:TPU:0, one launch (start us, length us, event | category | flops | bytes accessed | tf_op | source)
XLA Modules:
  0.0 65.3 jit_solution(487716962545357005)
XLA Ops:
  0.6 49.5 %shard_map.59 = (bf16[256,2048]{1,0:T(8,128)(2,1)}, bf16[256,2048]{1,0:T(8,128)(2,1)}, f32[8,48,128]{2,1,0:T(8,128)}) custom-call(bf16[256,16,128]{2,1,0:T(8,128)(2,1)} %frame_ref.1, s32[256,16,128]{2,1,0:T(8,128)} %mask_ref.1, s32[16,128]{1,0:T(8,128)} %good_ref.1, f32[128,128]{1,0:T(8,128)} %constant.2.clone.w_ref), custom_call_target="tpu_custom_call" | custom-call | tf_op jit(solution)/shard_map/pallas_call | solution.py:237
  50.1 15.1 %shard_map.60 = (f32[256,256]{1,0:T(8,128)}, bf16[4096,128]{1,0:T(8,128)(2,1)}) custom-call(f32[3,128,128]{2,1,0:T(8,128)} %bitcast.2, bf16[256,2048]{1,0:T(8,128)(2,1)} %get-tuple-element.8.hi_ref, bf16[256,2048]{1,0:T(8,128)(2,1)} %get-tuple-element.9.lo_ref), custom_call_target="tpu_custom_call" | custom-call | tf_op jit(solution)/shard_map/pallas_call | solution.py:291

commit v5 on v4

--- a/solution.py
+++ b/solution.py
@@ -111,7 +111,7 @@
     return out
 
 
-CHUNKS = 4
+CHUNKS = 8
 
 
 def exchange_kernel(ccds, tiles, tile_rows, frame_ref, mask_ref, good_ref, w_ref, hi_ref, lo_ref, o_ref, own_ref, halo, pad, done, mine,

time: 65.4 us -> 64.8 us (level)
    pallas_call x1, Pallas kernels: 49.5 us -> 48.7 us  [exchange(): pl.pallas_call(functools.partial(exchange_kernel, ccds, tiles, tile_rows)...]
where the time goes in v5:
time: 64.8 us; the launch traced here: 64.6 us
  Pallas kernels  64 us (99%)
    pallas_call x1, Pallas kernels, exchange(): pl.pallas_call(functools.partial(exchange_kernel, ccds, tiles, tile_rows)...  48.7 us
    pallas_call x1, Pallas kernels, solve(): pl.pallas_call(functools.partial(solve_kernel, pixel_total), out_shape=(j...  15.3 us

profile of v5, /device:TPU:0, one launch (start us, length us, event | category | flops | bytes accessed | tf_op | source)
XLA Modules:
  0.0 64.6 jit_solution(9733851553925176559)
XLA Ops:
  0.6 48.7 %shard_map.59 = (bf16[256,2048]{1,0:T(8,128)(2,1)}, bf16[256,2048]{1,0:T(8,128)(2,1)}, f32[8,48,128]{2,1,0:T(8,128)}) custom-call(bf16[256,16,128]{2,1,0:T(8,128)(2,1)} %frame_ref.1, s32[256,16,128]{2,1,0:T(8,128)} %mask_ref.1, s32[16,128]{1,0:T(8,128)} %good_ref.1, f32[128,128]{1,0:T(8,128)} %constant.2.clone.w_ref), custom_call_target="tpu_custom_call" | custom-call | tf_op jit(solution)/shard_map/pallas_call | solution.py:237
  49.3 15.3 %shard_map.60 = (f32[256,256]{1,0:T(8,128)}, bf16[4096,128]{1,0:T(8,128)(2,1)}) custom-call(f32[3,128,128]{2,1,0:T(8,128)} %bitcast.2, bf16[256,2048]{1,0:T(8,128)(2,1)} %get-tuple-element.8.hi_ref, bf16[256,2048]{1,0:T(8,128)(2,1)} %get-tuple-element.9.lo_ref), custom_call_target="tpu_custom_call" | custom-call | tf_op jit(solution)/shard_map/pallas_call | solution.py:291
